TPU v7x, 512 devices: a whole 4x4x16 slice. The times are simulated.
512 devices in a mesh: chain: 32 (over y, z_lo, core), block: 16 (over z_hi, x).
Axes of the slice: x: 4, y: 4, z: 16 (z_hi: 4, z_lo: 4; z = z_hi * 4 + z_lo), core: 2. Of those that a mesh axis runs over, the one named last changes fastest.
Arguments:
- state: bfloat16 [32, 16, 512, 512], P('chain', 'block'), may hold values from -400 to 400
- left_env: bfloat16 [32, 16, 2, 512, 512], P('chain', 'block'), may hold values from -1 to 5
- right_env: bfloat16 [32, 16, 2, 512, 512], P('chain', 'block'), may hold values from -1 to 5
- precond: float32 [32, 16, 512, 512], P('chain', 'block'), may hold values from 0.2 to 1
- ranks: int32 [32], P('chain'), may hold values from 1024 to 2048
Outputs:
- bond_out: bfloat16 [32, 16, 512, 512], P('chain', 'block')
All inputs are finite; a program needn't handle non-finite values.
Results may differ from a plain program's by a relative error of at most 0.0063.
Values may be sent and summed in bfloat16 or wider, within the bound.
No kernel may reach another device: no remote copies, remote signals or barrier semaphores. Data moves between devices by JAX's collectives and lax.ppermute only.
A program may use at most 64 MiB of HBM per device.

v0:
```python
import math

import jax
import jax.numpy as jnp
from jax import lax
from jax.sharding import Mesh
from jax.sharding import PartitionSpec as P

BLOCK = ("block_0", "block_1")


def from_partner(value, axis, distance):
    mask = 2**distance
    pairs = [(source, source ^ mask) for source in range(lax.axis_size(axis))]
    return lax.ppermute(value, axis, pairs)


def one_axis_at_a_time(x, axes):
    for axis in axes:
        x = lax.psum(x, axis)
    return x


def from_behind(value, axis, steps):
    count = lax.axis_size(axis)
    pairs = [(source, (source + steps) % count) for source in range(count)]
    return lax.ppermute(value, axis, pairs)


def join_halves(gathered, partner, position, bit_number, along):
    lower_half = position >> bit_number & 1 == 0
    first_way = jnp.concatenate([gathered, partner], along)
    second_way = jnp.concatenate([partner, gathered], along)
    return jnp.where(lower_half, first_way, second_way)


def unreverse(gathered, along, levels):
    shape = gathered.shape
    split_shape = shape[:along] + (2,) * levels + (shape[along] // 2**levels,) + shape[along + 1 :]
    order = (
        list(range(along))
        + list(range(along + levels - 1, along - 1, -1))
        + list(range(along + levels, len(split_shape)))
    )
    return gathered.reshape(split_shape).transpose(order).reshape(shape)


def gather_state_rows(gathered, position, levels):
    for level in range(levels):
        partner = from_partner(gathered, BLOCK, level)
        gathered = join_halves(gathered, partner, position, level, 1)
    return gathered


def gather_left_rows(gathered, position, levels):
    for level in range(levels):
        partner = from_partner(gathered, BLOCK, level)
        gathered = join_halves(gathered, partner, position, level, 2)
    return gathered


def gather_right_cols(gathered, position, levels):
    for level in range(levels):
        partner = from_partner(gathered, BLOCK, levels + level)
        gathered = join_halves(gathered, partner, position, levels + level, 1)
    return gathered


def gather_mid_cols(gathered, position, levels):
    level_order = list(range(levels - 1, -1, -1))
    for level in level_order:
        partner = from_partner(gathered, BLOCK, levels + level)
        gathered = join_halves(gathered, partner, position, levels + level, 1)
    gathered = unreverse(gathered, 1, levels)
    return gathered


def mix_weighted(first_tile, second_tile, first_weight, second_weight):
    return (
        first_weight * first_tile.astype(jnp.float32)
        + second_weight * second_tile.astype(jnp.float32)
    ).astype(jnp.bfloat16)


def per_device(state, left_env, right_env, precond, ranks):
    grid_side = math.isqrt(lax.axis_size(BLOCK))
    levels = grid_side.bit_length() - 1
    position = lax.axis_index(BLOCK)
    state_tile = state[0, 0]
    left_tiles = left_env[0, 0]
    right_tiles = right_env[0, 0]
    scaling = precond[0, 0]
    width = state_tile.shape[0]
    order_full = grid_side * width
    state_rows = gather_state_rows(state_tile, position, levels)
    left_rows = gather_left_rows(left_tiles, position, levels)
    right_cols = gather_right_cols(right_tiles, position, levels)
    middle = jnp.einsum(
        "ij,kjl->kil", state_rows, right_cols, preferred_element_type=jnp.float32
    ).astype(jnp.bfloat16)
    middle_cols = gather_mid_cols(middle, position, levels)
    image = jnp.einsum("kij,kjl->il", left_rows, middle_cols, preferred_element_type=jnp.float32)
    state_f = state_tile.astype(jnp.float32)
    row_index = position // grid_side * width + jnp.arange(width, dtype=jnp.int32)
    col_index = position % grid_side * width + jnp.arange(width, dtype=jnp.int32)
    rank_limit = ranks[0]
    keep_mask = ((row_index[:, None] < rank_limit) & (col_index[None, :] < rank_limit)).astype(
        jnp.float32
    )
    total_count = float(order_full * order_full)
    weighted = keep_mask * scaling
    state_sq = state_f * state_f
    cross_term = state_f * image
    moment_terms = (
        jnp.sum(state_sq),
        jnp.sum(cross_term),
        jnp.sum(keep_mask * state_sq),
        jnp.sum(weighted * state_sq),
        jnp.sum(weighted * scaling * state_sq),
        jnp.sum(weighted * cross_term),
        jnp.sum(weighted * scaling * cross_term),
        jnp.sum(weighted * scaling * image * image),
    )
    norm_state, intersection, plain_sq, first_sq, second_sq, first_cross, second_cross, image_sq = (
        one_axis_at_a_time(moment_terms[0], BLOCK),
        one_axis_at_a_time(moment_terms[1], BLOCK),
        one_axis_at_a_time(moment_terms[2], BLOCK),
        one_axis_at_a_time(moment_terms[3], BLOCK),
        one_axis_at_a_time(moment_terms[4], BLOCK),
        one_axis_at_a_time(moment_terms[5], BLOCK),
        one_axis_at_a_time(moment_terms[6], BLOCK),
        one_axis_at_a_time(moment_terms[7], BLOCK),
    )
    energy = intersection / norm_state
    corrected = keep_mask * (state_f - (image - energy * state_f) * scaling)
    square_sum = (
        plain_sq
        + 2.0 * energy * first_sq
        + energy * energy * second_sq
        - 2.0 * first_cross
        - 2.0 * energy * second_cross
        + image_sq
    )
    bond = (corrected / jnp.sqrt(square_sum / total_count + 1e-06)).astype(jnp.bfloat16)
    partner = from_partner(bond, "chain", 0)
    own_pair = mix_weighted(bond, partner, 0.75, 0.25)
    ahead = from_behind(own_pair, "chain", -1)
    crossed = from_partner(ahead, "chain", 0)
    other_pair = from_behind(crossed, "chain", 1)
    result = mix_weighted(own_pair, other_pair, 0.5, 0.5)
    return result[None, None]


def solution(mesh):
    split = Mesh(mesh.devices.reshape(mesh.shape["chain"], 4, 4), ("chain", "block_0", "block_1"))
    placed = (
        P("chain", BLOCK, None, None),
        P("chain", BLOCK, None, None, None),
        P("chain", BLOCK, None, None, None),
        P("chain", BLOCK, None, None),
        P("chain"),
    )
    return jax.shard_map(
        per_device,
        mesh=split,
        in_specs=placed,
        out_specs=P("chain", BLOCK, None, None),
        check_vma=False,
    )
```

profile of v0, /device:TPU:2, one launch (start us, length us, event | category | flops | bytes accessed | tf_op | source)
XLA Modules:
  0.0 672.2 jit_solution(9116957013693709141)
XLA Ops:
  0.0 0.0 copy-start
  0.0 9.2 %collective-permute-start.2 = (bf16[2,512,512]{2,1,0:T(8,128)(2,1)}, bf16[2,512,512]{2,1,0:T(8,128)(2,1)}, u32[]{:S(2)}, u32[]{:S(2)}) collective-permute-start(bf16[2,512,512]{2,1,0:T(8,128)(2,1)} %bitcast.46), channel_id=1, source_target_pairs={{0,4},{1,5},{2,6},{3,7},{4,0},{5,1},{6,2},{7,3},{8,12},{9,13},{10,... | collective-permute-start | bytes 3145736 | tf_op jit(solution)/shard_map/ppermute | solution.py:15
  9.2 136.1 %collective-permute-done.2 = bf16[2,512,512]{2,1,0:T(8,128)(2,1)} collective-permute-done((bf16[2,512,512]{2,1,0:T(8,128)(2,1)}, bf16[2,512,512]{2,1,0:T(8,128)(2,1)}, u32[]{:S(2)}, u32[]{:S(2)}) %collective-permute-start.2) | collective-permute-done | bytes 1048608 | tf_op jit(solution)/shard_map/ppermute | solution.py:15
  145.3 2.8 maximum_select_fusion.7
  148.2 127.8 %collective-permute-start.3 = (bf16[2,1024,512]{2,1,0:T(8,128)(2,1)S(1)}, bf16[2,1024,512]{2,1,0:T(8,128)(2,1)}, u32[]{:S(2)}, u32[]{:S(2)}) collective-permute-start(bf16[2,1024,512]{2,1,0:T(8,128)(2,1)S(1)} %maximum_select_fusion.7), channel_id=1, source_target_pairs={{0,8},{1,9},{2,10},{3,11},{4,12},{5,13},{6,14},{7,15},{8,0},{9,1},... | collective-permute-start | bytes 6291464 | tf_op jit(solution)/shard_map/ppermute | solution.py:15
  276.0 0.0 copy-done
  276.0 2.4 collective-permute-start.4
  278.5 12.5 %collective-permute-done.4 = bf16[512,512]{1,0:T(8,128)(2,1)S(1)} collective-permute-done((bf16[512,512]{1,0:T(8,128)(2,1)S(1)}, bf16[512,512]{1,0:T(8,128)(2,1)S(1)}, u32[]{:S(2)}, u32[]{:S(2)}) %collective-permute-start.4) | collective-permute-done | bytes 524320 | tf_op jit(solution)/shard_map/ppermute | solution.py:15
  291.0 1.3 maximum_select_fusion.15
  292.3 4.0 collective-permute-start.5
  296.3 0.0 copy-start.1
  296.3 23.2 %collective-permute-done.5 = bf16[512,1024]{1,0:T(8,128)(2,1)} collective-permute-done((bf16[512,1024]{1,0:T(8,128)(2,1)}, bf16[512,1024]{1,0:T(8,128)(2,1)}, u32[]{:S(2)}, u32[]{:S(2)}) %collective-permute-start.5) | collective-permute-done | bytes 1048608 | tf_op jit(solution)/shard_map/ppermute | solution.py:15
  319.6 2.2 collective-permute-done.3
  321.8 5.9 fusion.29
  327.6 12.2 %collective-permute-start.6 = (bf16[2,512,512]{2,1,0:T(8,128)(2,1)S(1)}, bf16[2,512,512]{2,1,0:T(8,128)(2,1)S(1)}, u32[]{:S(2)}, u32[]{:S(2)}) collective-permute-start(bf16[2,512,512]{2,1,0:T(8,128)(2,1)S(1)} %fusion.29), channel_id=1, source_target_pairs={{0,8},{1,9},{2,10},{3,11},{4,12},{5,13},{6,14},{7,15},{8,0},{9,1},... | collective-permute-start | bytes 3145736 | tf_op jit(solution)/shard_map/ppermute | solution.py:15
  339.9 0.0 copy-done.1
  339.9 2.4 collective-permute-start
  342.4 19.9 %collective-permute-done.6 = bf16[2,512,512]{2,1,0:T(8,128)(2,1)S(1)} collective-permute-done((bf16[2,512,512]{2,1,0:T(8,128)(2,1)S(1)}, bf16[2,512,512]{2,1,0:T(8,128)(2,1)S(1)}, u32[]{:S(2)}, u32[]{:S(2)}) %collective-permute-start.6) | collective-permute-done | bytes 1048608 | tf_op jit(solution)/shard_map/ppermute | solution.py:15
  362.2 0.7 maximum_select_fusion.8
  362.9 170.4 %collective-permute-start.7 = (bf16[2,1024,512]{2,1,0:T(8,128)(2,1)S(1)}, bf16[2,1024,512]{2,1,0:T(8,128)(2,1)}, u32[]{:S(2)}, u32[]{:S(2)}) collective-permute-start(bf16[2,1024,512]{2,1,0:T(8,128)(2,1)S(1)} %maximum_select_fusion.8), channel_id=1, source_target_pairs={{0,4},{1,5},{2,6},{3,7},{4,0},{5,1},{6,2},{7,3},{8,12},{9,13},{10,... | collective-permute-start | bytes 6291464 | tf_op jit(solution)/shard_map/ppermute | solution.py:15
  533.4 0.0 collective-permute-done
  533.4 2.0 maximum_select_fusion.5
  535.4 4.0 collective-permute-start.1
  540.1 39.1 %collective-permute-done.7 = bf16[2,1024,512]{2,1,0:T(8,128)(2,1)} collective-permute-done((bf16[2,1024,512]{2,1,0:T(8,128)(2,1)S(1)}, bf16[2,1024,512]{2,1,0:T(8,128)(2,1)}, u32[]{:S(2)}, u32[]{:S(2)}) %collective-permute-start.7) | collective-permute-done | bytes 2097184 | tf_op jit(solution)/shard_map/ppermute | solution.py:15
  579.2 3.3 maximum_select_fusion.4
  582.5 0.0 copy-start.2
  582.5 0.3 copy.6
  582.8 3.5 collective-permute-done.1
  586.3 0.0 copy-done.2
  586.3 5.9 multiply_reduce_fusion
  592.1 14.3 %all-reduce.1 = (f32[]{:T(128)}, f32[]{:T(128)}, f32[]{:T(128)}, f32[]{:T(128)}, f32[]{:T(128)}, /*index=5*/f32[]{:T(128)}, f32[]{:T(128)}, f32[]{:T(128)}) all-reduce(f32[]{:T(128)} %get-tuple-element.11, f32[]{:T(128)} %get-tuple-element.10, f32[]{:T(128)} %get-tuple-element.12, ...), channel_id=1, replica_groups=mesh['chain'=32,'block_0'=4,'block_1'=4] {'block_0'}, use_global_device_ids=true, to_apply=%region_7.8 | all-reduce | flops 8 | bytes 64 | tf_op jit(solution)/shard_map/psum | solution.py:20
  606.5 9.3 %all-reduce = (f32[]{:T(128)}, f32[]{:T(128)}, f32[]{:T(128)}, f32[]{:T(128)}, f32[]{:T(128)}, /*index=5*/f32[]{:T(128)}, f32[]{:T(128)}, f32[]{:T(128)}) all-reduce(f32[]{:T(128)} %get-tuple-element.21, f32[]{:T(128)} %get-tuple-element.22, f32[]{:T(128)} %get-tuple-element.23, ...), channel_id=1, replica_groups=mesh['chain'=32,'block_0'=4,'block_1'=4] {'block_1'}, use_global_device_ids=true, to_apply=%region_8.9 | all-reduce | flops 8 | bytes 64 | tf_op jit(solution)/shard_map/psum | solution.py:20
  621.0 0.3 fusion.38
  621.3 1.9 collective-permute-start.8
  623.2 1.9 collective-permute-done.8
  625.1 0.2 add_convert_fusion
  625.3 20.9 %collective-permute-start.9 = (bf16[512,512]{1,0:T(8,128)(2,1)S(1)}, bf16[512,512]{1,0:T(8,128)(2,1)S(1)}, u32[]{:S(2)}, u32[]{:S(2)}) collective-permute-start(bf16[512,512]{1,0:T(8,128)(2,1)S(1)} %add_convert_fusion), channel_id=1, source_target_pairs={{0,496},{16,0},{32,16},{48,32},{64,48},{80,64},{96,80},{112,96},{1... | collective-permute-start | bytes 1572872 | tf_op jit(solution)/shard_map/ppermute | solution.py:27
  646.2 6.7 collective-permute-done.9
  652.9 1.9 collective-permute-start.10
  654.8 1.9 collective-permute-done.10
  656.7 2.0 collective-permute-start.11
  658.7 12.5 %collective-permute-done.11 = bf16[512,512]{1,0:T(8,128)(2,1)S(1)} collective-permute-done((bf16[512,512]{1,0:T(8,128)(2,1)S(1)}, bf16[512,512]{1,0:T(8,128)(2,1)S(1)}, u32[]{:S(2)}, u32[]{:S(2)}) %collective-permute-start.11) | collective-permute-done | bytes 524320 | tf_op jit(solution)/shard_map/ppermute | solution.py:27
  671.3 1.0 fusion.44
  (1 shorter events, 0.0 us)
Async XLA Ops:
  0.0 276.0 %copy-start = (bf16[1,1,512,512]{3,2,1,0:T(8,128)(2,1)S(1)}, bf16[1,1,512,512]{3,2,1,0:T(8,128)(2,1)}, u32[]{:S(2)}) copy-start(bf16[1,1,512,512]{3,2,1,0:T(8,128)(2,1)} %param.5) | copy-start | bytes 1572868
  0.0 145.3 %collective-permute-start.2 = (bf16[2,512,512]{2,1,0:T(8,128)(2,1)}, bf16[2,512,512]{2,1,0:T(8,128)(2,1)}, u32[]{:S(2)}, u32[]{:S(2)}) collective-permute-start(bf16[2,512,512]{2,1,0:T(8,128)(2,1)} %bitcast.46), channel_id=1, source_target_pairs={{0,4},{1,5},{2,6},{3,7},{4,0},{5,1},{6,2},{7,3},{8,12},{9,13},{10,... | collective-permute-start | bytes 3145736 | tf_op jit(solution)/shard_map/ppermute | solution.py:15
  148.2 173.6 %collective-permute-start.3 = (bf16[2,1024,512]{2,1,0:T(8,128)(2,1)S(1)}, bf16[2,1024,512]{2,1,0:T(8,128)(2,1)}, u32[]{:S(2)}, u32[]{:S(2)}) collective-permute-start(bf16[2,1024,512]{2,1,0:T(8,128)(2,1)S(1)} %maximum_select_fusion.7), channel_id=1, source_target_pairs={{0,8},{1,9},{2,10},{3,11},{4,12},{5,13},{6,14},{7,15},{8,0},{9,1},... | collective-permute-start | bytes 6291464 | tf_op jit(solution)/shard_map/ppermute | solution.py:15
  276.0 15.0 %collective-permute-start.4 = (bf16[512,512]{1,0:T(8,128)(2,1)S(1)}, bf16[512,512]{1,0:T(8,128)(2,1)S(1)}, u32[]{:S(2)}, u32[]{:S(2)}) collective-permute-start(bf16[512,512]{1,0:T(8,128)(2,1)S(1)} %bitcast.44), channel_id=1, source_target_pairs={{0,1},{1,0},{2,3},{3,2},{4,5},{5,4},{6,7},{7,6},{8,9},{9,8},{10,11... | collective-permute-start | bytes 1572872 | tf_op jit(solution)/shard_map/ppermute | solution.py:15
  292.3 27.3 %collective-permute-start.5 = (bf16[512,1024]{1,0:T(8,128)(2,1)}, bf16[512,1024]{1,0:T(8,128)(2,1)}, u32[]{:S(2)}, u32[]{:S(2)}) collective-permute-start(bf16[512,1024]{1,0:T(8,128)(2,1)} %maximum_select_fusion.15), channel_id=1, source_target_pairs={{0,2},{1,3},{2,0},{3,1},{4,6},{5,7},{6,4},{7,5},{8,10},{9,11},{10,... | collective-permute-start | bytes 3145736 | tf_op jit(solution)/shard_map/ppermute | solution.py:15
  296.3 43.6 %copy-start.1 = (bf16[1,1,2,512,512]{4,3,2,1,0:T(8,128)(2,1)S(1)}, bf16[1,1,2,512,512]{4,3,2,1,0:T(8,128)(2,1)}, u32[]{:S(2)}) copy-start(bf16[1,1,2,512,512]{4,3,2,1,0:T(8,128)(2,1)} %param.6) | copy-start | bytes 3145732
  327.6 34.6 %collective-permute-start.6 = (bf16[2,512,512]{2,1,0:T(8,128)(2,1)S(1)}, bf16[2,512,512]{2,1,0:T(8,128)(2,1)S(1)}, u32[]{:S(2)}, u32[]{:S(2)}) collective-permute-start(bf16[2,512,512]{2,1,0:T(8,128)(2,1)S(1)} %fusion.29), channel_id=1, source_target_pairs={{0,8},{1,9},{2,10},{3,11},{4,12},{5,13},{6,14},{7,15},{8,0},{9,1},... | collective-permute-start | bytes 3145736 | tf_op jit(solution)/shard_map/ppermute | solution.py:15
  339.9 193.5 %collective-permute-start = (bf16[2,512,512]{2,1,0:T(8,128)(2,1)S(1)}, bf16[2,512,512]{2,1,0:T(8,128)(2,1)S(1)}, u32[]{:S(2)}, u32[]{:S(2)}) collective-permute-start(bf16[2,512,512]{2,1,0:T(8,128)(2,1)S(1)} %bitcast.48), channel_id=1, source_target_pairs={{0,1},{1,0},{2,3},{3,2},{4,5},{5,4},{6,7},{7,6},{8,9},{9,8},{10,11... | collective-permute-start | bytes 3145736 | tf_op jit(solution)/shard_map/ppermute | solution.py:15
  362.9 216.2 %collective-permute-start.7 = (bf16[2,1024,512]{2,1,0:T(8,128)(2,1)S(1)}, bf16[2,1024,512]{2,1,0:T(8,128)(2,1)}, u32[]{:S(2)}, u32[]{:S(2)}) collective-permute-start(bf16[2,1024,512]{2,1,0:T(8,128)(2,1)S(1)} %maximum_select_fusion.8), channel_id=1, source_target_pairs={{0,4},{1,5},{2,6},{3,7},{4,0},{5,1},{6,2},{7,3},{8,12},{9,13},{10,... | collective-permute-start | bytes 6291464 | tf_op jit(solution)/shard_map/ppermute | solution.py:15
  535.4 50.9 %collective-permute-start.1 = (bf16[2,512,1024]{2,1,0:T(8,128)(2,1)}, bf16[2,512,1024]{2,1,0:T(8,128)(2,1)}, u32[]{:S(2)}, u32[]{:S(2)}) collective-permute-start(bf16[2,512,1024]{2,1,0:T(8,128)(2,1)} %maximum_select_fusion.5), channel_id=1, source_target_pairs={{0,2},{1,3},{2,0},{3,1},{4,6},{5,7},{6,4},{7,5},{8,10},{9,11},{10,... | collective-permute-start | bytes 6291464 | tf_op jit(solution)/shard_map/ppermute | solution.py:15
  582.5 3.8 copy-start.2
  621.3 3.8 collective-permute-start.8
  625.3 27.6 %collective-permute-start.9 = (bf16[512,512]{1,0:T(8,128)(2,1)S(1)}, bf16[512,512]{1,0:T(8,128)(2,1)S(1)}, u32[]{:S(2)}, u32[]{:S(2)}) collective-permute-start(bf16[512,512]{1,0:T(8,128)(2,1)S(1)} %add_convert_fusion), channel_id=1, source_target_pairs={{0,496},{16,0},{32,16},{48,32},{64,48},{80,64},{96,80},{112,96},{1... | collective-permute-start | bytes 1572872 | tf_op jit(solution)/shard_map/ppermute | solution.py:27
  652.9 3.8 collective-permute-start.10
  656.7 14.6 %collective-permute-start.11 = (bf16[512,512]{1,0:T(8,128)(2,1)S(1)}, bf16[512,512]{1,0:T(8,128)(2,1)S(1)}, u32[]{:S(2)}, u32[]{:S(2)}) collective-permute-start(bf16[512,512]{1,0:T(8,128)(2,1)S(1)} %collective-permute-done.10), channel_id=1, source_target_pairs={{0,16},{16,32},{32,48},{48,64},{64,80},{80,96},{96,112},{112,128},... | collective-permute-start | bytes 1572872 | tf_op jit(solution)/shard_map/ppermute | solution.py:27
where the time goes:
time: 673 us; the launch traced here: 672 us
  starting transfers between devices  359 us (53%)
  waiting for transfers between devices  259 us (38%)
  blocking collectives  23.6 us (4%)
  matrix products  11.7 us (2%)
  other arithmetic  11.6 us (2%)
    ppermute x10, starting transfers between devices, from_partner(): return lax.ppermute(value, axis, pairs)  336 us
    ppermute x10, waiting for transfers between devices, from_partner(): return lax.ppermute(value, axis, pairs)  240 us
    psum x2, blocking collectives, one_axis_at_a_time(): x = lax.psum(x, axis)  23.6 us
    ppermute x2, starting transfers between devices, from_behind(): return lax.ppermute(value, axis, pairs)  23 us
    ppermute x2, waiting for transfers between devices, from_behind(): return lax.ppermute(value, axis, pairs)  19.2 us
  transfers between devices with their start and end apart: 12, of which 11 were waited for; matrix products, arithmetic and copies ran while one was open for 1% of the time, Pallas kernels for 0%

commit v1 on v0

v1 whole, which is shorter than its diff:
```python
import jax
import jax.numpy as jnp
from jax import lax
from jax.sharding import Mesh
from jax.sharding import PartitionSpec as P


BLOCK = ("block_0", "block_1")


def shift(value, axis, steps):
    count = lax.axis_size(axis)
    pairs = [(source, (source + steps) % count) for source in range(count)]
    return lax.ppermute(value, axis, pairs)


def even_partner(value):
    pairs = [(source, source ^ 1) for source in range(lax.axis_size("chain"))]
    return lax.ppermute(value, "chain", pairs)


def odd_partner(value):
    count = lax.axis_size("chain")
    pairs = [(source, (source + (1 if source % 2 else -1)) % count) for source in range(count)]
    return lax.ppermute(value, "chain", pairs)


def ring_pieces(value, axis):
    half = value.shape[-2] // 2
    behind = shift(value, axis, 1)
    ahead = shift(value, axis, -1)
    top = shift(behind[..., :half, :], axis, 1)
    bottom = shift(ahead[..., half:, :], axis, -1)
    return [value, behind, jnp.concatenate([top, bottom], axis=-2), ahead]


def mix_weighted(first_tile, second_tile, first_weight, second_weight):
    return (
        first_weight * first_tile.astype(jnp.float32)
        + second_weight * second_tile.astype(jnp.float32)
    ).astype(jnp.bfloat16)


def one_window(state, left_env, right_env, precond, ranks):
    side = lax.axis_size("block_0")
    row = lax.axis_index("block_0")
    col = lax.axis_index("block_1")
    state_tile = state[0, 0]
    left_tiles = left_env[0, 0]
    right_tiles = right_env[0, 0]
    scaling = precond[0, 0]
    terms = left_tiles.shape[0]
    width = state_tile.shape[0]
    order_full = side * width

    left_rows = lax.all_gather(left_tiles, "block_1", axis=0)
    state_pieces = ring_pieces(state_tile, "block_0")
    right_pieces = ring_pieces(right_tiles, "block_0")

    def block_of(gathered, distance):
        return lax.dynamic_index_in_dim(gathered, (row - distance) % side, 0, keepdims=False)

    partial = jnp.zeros((terms, width, width), jnp.float32)
    for distance in (0, 1, 3, 2):
        partial = partial + jnp.einsum(
            "kij,jl->kil",
            block_of(left_rows, distance),
            state_pieces[distance],
            preferred_element_type=jnp.float32,
        )
    turned_rows = lax.all_gather(partial.astype(jnp.bfloat16), "block_1", axis=0)
    image = jnp.zeros((width, width), jnp.float32)
    for distance in (0, 1, 3, 2):
        image = image + jnp.einsum(
            "kij,kjl->il",
            block_of(turned_rows, distance),
            right_pieces[distance],
            preferred_element_type=jnp.float32,
        )

    state_f = state_tile.astype(jnp.float32)
    row_index = row * width + jnp.arange(width, dtype=jnp.int32)
    col_index = col * width + jnp.arange(width, dtype=jnp.int32)
    rank_limit = ranks[0]
    keep_mask = ((row_index[:, None] < rank_limit) & (col_index[None, :] < rank_limit)).astype(
        jnp.float32
    )
    total_count = float(order_full * order_full)
    weighted = keep_mask * scaling
    state_sq = state_f * state_f
    cross_term = state_f * image
    moments = jnp.stack(
        [
            jnp.sum(state_sq),
            jnp.sum(cross_term),
            jnp.sum(keep_mask * state_sq),
            jnp.sum(weighted * state_sq),
            jnp.sum(weighted * scaling * state_sq),
            jnp.sum(weighted * cross_term),
            jnp.sum(weighted * scaling * cross_term),
            jnp.sum(weighted * scaling * image * image),
        ]
    )
    for axis in BLOCK:
        moments = lax.psum(moments, axis)
    norm_state, intersection, plain_sq, first_sq, second_sq, first_cross, second_cross, image_sq = (
        moments[index] for index in range(8)
    )
    energy = intersection / norm_state
    corrected = keep_mask * (state_f - (image - energy * state_f) * scaling)
    square_sum = (
        plain_sq
        + 2.0 * energy * first_sq
        + energy * energy * second_sq
        - 2.0 * first_cross
        - 2.0 * energy * second_cross
        + image_sq
    )
    bond = (corrected / jnp.sqrt(square_sum / total_count + 1e-06)).astype(jnp.bfloat16)
    own_pair = mix_weighted(bond, even_partner(bond), 0.75, 0.25)
    result = mix_weighted(own_pair, odd_partner(own_pair), 0.5, 0.5)
    return result[None, None]


def solution(mesh):
    split = Mesh(mesh.devices.reshape(mesh.shape["chain"], 4, 4), ("chain", "block_0", "block_1"))
    placed = (
        P("chain", BLOCK, None, None),
        P("chain", BLOCK, None, None, None),
        P("chain", BLOCK, None, None, None),
        P("chain", BLOCK, None, None),
        P("chain"),
    )
    return jax.shard_map(
        one_window,
        mesh=split,
        in_specs=placed,
        out_specs=P("chain", BLOCK, None, None),
        check_vma=False,
    )
```

time: 673 us -> 319 us (0.47)
  the two profiles are of different devices: /device:TPU:2 before, /device:TPU:1 now
where the time goes in v1:
time: 319 us; the launch traced here: 318 us
  waiting for transfers between devices  125 us (39%)
  starting transfers between devices  118 us (37%)
  blocking collectives  32.5 us (10%)
  between operations  19.4 us (6%)
  matrix products  15.2 us (5%)
  local copies, waits for them, and re-layouts  6.89 us (2%)
    ppermute x8, starting transfers between devices, shift(): return lax.ppermute(value, axis, pairs)  103 us
    ppermute x8, waiting for transfers between devices, shift(): return lax.ppermute(value, axis, pairs)  102 us
    psum x2, blocking collectives, one_window(): moments = lax.psum(moments, axis)  32.5 us
    ppermute x1, waiting for transfers between devices, odd_partner(): return lax.ppermute(value, 'chain', pairs)  14.2 us
    ppermute x1, starting transfers between devices, even_partner(): return lax.ppermute(value, 'chain', pairs)  12.4 us
    dot_general x4, matrix products, one_window(): jnp.einsum('kij,kjl->il', block_of(turned_rows, distance), right_pieces[d...  8.7 us
    all_gather x1, waiting for transfers between devices, one_window(): lax.all_gather(partial.astype(jnp.bfloat16), 'block_1', axis=0)  7.17 us
    dot_general x4, matrix products, one_window(): jnp.einsum('kij,jl->kil', block_of(left_rows, distance), state_pieces[dis...  6.45 us
  transfers between devices with their start and end apart: 12, of which 9 were waited for; matrix products, arithmetic and copies ran while one was open for 3% of the time, Pallas kernels for 0%

profile of v1, /device:TPU:1, one launch (start us, length us, event | category | flops | bytes accessed | tf_op | source)
XLA Modules:
  0.0 318.4 jit_solution(12058377247817040268)
XLA Ops:
  6.5 0.0 all-gather.5.cloned.1.call-start
  6.5 0.7 all-gather.5.cloned.1.call-update
  7.3 0.0 all-gather.7.cloned.1.call-start
  7.3 9.6 %collective-permute-start = (bf16[512,512]{1,0:T(8,128)(2,1)}, bf16[512,512]{1,0:T(8,128)(2,1)S(1)}, u32[]{:S(2)}, u32[]{:S(2)}) collective-permute-start(bf16[512,512]{1,0:T(8,128)(2,1)} %bitcast.100), channel_id=1, source_target_pairs={{0,4},{4,8},{8,12},{12,0},{1,5},{5,9},{9,13},{13,1},{2,6},{6,10},{... | collective-permute-start | bytes 1572872 | tf_op jit(solution)/shard_map/ppermute | solution.py:14
  16.9 5.6 %collective-permute-start.1 = (bf16[512,512]{1,0:T(8,128)(2,1)}, bf16[512,512]{1,0:T(8,128)(2,1)S(1)}, u32[]{:S(2)}, u32[]{:S(2)}) collective-permute-start(bf16[512,512]{1,0:T(8,128)(2,1)} %bitcast.101), channel_id=1, source_target_pairs={{0,12},{4,0},{8,4},{12,8},{1,13},{5,1},{9,5},{13,9},{2,14},{6,2},{... | collective-permute-start | bytes 1572872 | tf_op jit(solution)/shard_map/ppermute | solution.py:14
  22.6 0.0 copy-start.1
  22.6 15.9 %collective-permute-done = bf16[512,512]{1,0:T(8,128)(2,1)S(1)} collective-permute-done((bf16[512,512]{1,0:T(8,128)(2,1)}, bf16[512,512]{1,0:T(8,128)(2,1)S(1)}, u32[]{:S(2)}, u32[]{:S(2)}) %collective-permute-start) | collective-permute-done | bytes 524320 | tf_op jit(solution)/shard_map/ppermute | solution.py:14
  38.5 32.3 %collective-permute-start.2 = (bf16[256,512]{1,0:T(8,128)(2,1)S(1)}, bf16[256,512]{1,0:T(8,128)(2,1)S(1)}, u32[]{:S(2)}, u32[]{:S(2)}) collective-permute-start(bf16[256,512]{1,0:T(8,128)(2,1)S(1)} %slice.48), channel_id=1, source_target_pairs={{0,4},{4,8},{8,12},{12,0},{1,5},{5,9},{9,13},{13,1},{2,6},{6,10},{... | collective-permute-start | bytes 786440 | tf_op jit(solution)/shard_map/ppermute | solution.py:14
  70.8 0.9 collective-permute-done.1
  71.7 4.1 %collective-permute-start.3 = (bf16[256,512]{1,0:T(8,128)(2,1)S(1)}, bf16[256,512]{1,0:T(8,128)(2,1)S(1)}, u32[]{:S(2)}, u32[]{:S(2)}) collective-permute-start(bf16[256,512]{1,0:T(8,128)(2,1)S(1)} %slice.49), channel_id=1, source_target_pairs={{0,12},{4,0},{8,4},{12,8},{1,13},{5,1},{9,5},{13,9},{2,14},{6,2},{... | collective-permute-start | bytes 786440 | tf_op jit(solution)/shard_map/ppermute | solution.py:14
  75.8 0.0 all-gather.5.cloned.1.call-done
  75.8 0.0 copy-start
  75.9 2.1 fusion.29
  77.9 1.9 fusion.31
  79.9 0.0 copy-done.1
  79.9 0.0 copy-done
  79.9 0.7 fusion.33
  80.6 12.7 %collective-permute-done.2 = bf16[256,512]{1,0:T(8,128)(2,1)S(1)} collective-permute-done((bf16[256,512]{1,0:T(8,128)(2,1)S(1)}, bf16[256,512]{1,0:T(8,128)(2,1)S(1)}, u32[]{:S(2)}, u32[]{:S(2)}) %collective-permute-start.2) | collective-permute-done | bytes 262176 | tf_op jit(solution)/shard_map/ppermute | solution.py:14
  93.3 0.8 collective-permute-done.3
  94.1 1.7 add_convert_fusion
  95.8 0.0 all-gather.7.cloned.1.call-update
  95.8 40.5 %collective-permute-start.4 = (bf16[2,512,512]{2,1,0:T(8,128)(2,1)}, bf16[2,512,512]{2,1,0:T(8,128)(2,1)S(1)}, u32[]{:S(2)}, u32[]{:S(2)}) collective-permute-start(bf16[2,512,512]{2,1,0:T(8,128)(2,1)} %bitcast.106), channel_id=1, source_target_pairs={{0,4},{4,8},{8,12},{12,0},{1,5},{5,9},{9,13},{13,1},{2,6},{6,10},{... | collective-permute-start | bytes 3145736 | tf_op jit(solution)/shard_map/ppermute | solution.py:14
  136.3 1.9 collective-permute-start.5
  138.9 63.0 %collective-permute-done.4 = bf16[2,512,512]{2,1,0:T(8,128)(2,1)S(1)} collective-permute-done((bf16[2,512,512]{2,1,0:T(8,128)(2,1)}, bf16[2,512,512]{2,1,0:T(8,128)(2,1)S(1)}, u32[]{:S(2)}, u32[]{:S(2)}) %collective-permute-start.4) | collective-permute-done | bytes 1048608 | tf_op jit(solution)/shard_map/ppermute | solution.py:14
  201.9 0.0 copy-start.3
  202.0 3.0 collective-permute-start.6
  205.0 0.0 collective-permute-done.5
  205.0 1.1 slice.51
  206.1 6.2 %collective-permute-start.7 = (bf16[2,256,512]{2,1,0:T(8,128)(2,1)S(1)}, bf16[2,256,512]{2,1,0:T(8,128)(2,1)}, u32[]{:S(2)}, u32[]{:S(2)}) collective-permute-start(bf16[2,256,512]{2,1,0:T(8,128)(2,1)S(1)} %slice.51), channel_id=1, source_target_pairs={{0,12},{4,0},{8,4},{12,8},{1,13},{5,1},{9,5},{13,9},{2,14},{6,2},{... | collective-permute-start | bytes 1572872 | tf_op jit(solution)/shard_map/ppermute | solution.py:14
  212.3 7.2 %all-gather.7.cloned.1.call-done = bf16[8,512,512]{2,1,0:T(8,128)(2,1)} async-done(((bf16[2,512,512]{2,1,0:T(8,128)(2,1)}), bf16[8,512,512]{2,1,0:T(8,128)(2,1)}) %all-gather.7.cloned.1.call-update) | async-done | bytes 4194320 | tf_op jit(solution)/shard_map/all_gather | solution.py:71
  219.5 0.0 copy-start.5
  219.5 0.0 copy-done.3
  219.5 2.4 convolution_bitcast_fusion.3
  221.9 0.0 copy-start.2
  221.9 0.0 copy-start.4
  221.9 2.4 convolution_bitcast_fusion.1
  224.3 8.5 %collective-permute-done.6 = bf16[2,256,512]{2,1,0:T(8,128)(2,1)S(1)} collective-permute-done((bf16[2,256,512]{2,1,0:T(8,128)(2,1)S(1)}, bf16[2,256,512]{2,1,0:T(8,128)(2,1)S(1)}, u32[]{:S(2)}, u32[]{:S(2)}) %collective-permute-start.6) | collective-permute-done | bytes 524320 | tf_op jit(solution)/shard_map/ppermute | solution.py:14
  232.8 0.0 collective-permute-done.7
  232.8 0.0 copy-done.5
  232.8 1.8 convolution_bitcast_fusion
  234.6 0.0 copy-done.2
  234.6 0.0 copy-done.4
  234.6 2.2 multiply_reduce_fusion
  236.8 5.0 %stack.35 = f32[8]{0:T(128)S(1)} concatenate(f32[1]{0:T(128)} %bitcast.20, f32[1]{0:T(128)} %bitcast.21, f32[1]{0:T(128)} %bitcast.22, f32[1]{0:T(128)} %bitcast.24, f32[1]{0:T(128)} %bitcast.25, f32[1]{0:T(128)} %bitcast.26, f32[1]{0:T(128)} %bitcast.27, f32[1]{0:T(128)} %bitcast.28), dimensions={0} | concatenate | bytes 64 | tf_op jit(solution)/shard_map/stack | solution.py:92
  241.8 13.4 %psum.14 = f32[8]{0:T(128)S(1)} all-reduce(f32[8]{0:T(128)S(1)} %stack.35), channel_id=1, replica_groups=mesh['chain'=32,'block_0'=4,'block_1'=4] {'block_0'}, use_global_device_ids=true, to_apply=%region_8.9 | all-reduce | flops 8 | bytes 64 | tf_op jit(solution)/shard_map/psum | solution.py:105
  255.2 19.1 %psum.15 = f32[8]{0:T(128)S(1)} all-reduce(f32[8]{0:T(128)S(1)} %psum.14), channel_id=1, replica_groups=mesh['chain'=32,'block_0'=4,'block_1'=4] {'block_1'}, use_global_device_ids=true, to_apply=%region_9.10 | all-reduce | flops 8 | bytes 64 | tf_op jit(solution)/shard_map/psum | solution.py:105
  274.3 0.7 fusion.61
  280.0 0.4 fusion.12
  280.4 12.4 %collective-permute-start.8 = (bf16[512,512]{1,0:T(8,128)(2,1)S(1)}, bf16[512,512]{1,0:T(8,128)(2,1)S(1)}, u32[]{:S(2)}, u32[]{:S(2)}) collective-permute-start(bf16[512,512]{1,0:T(8,128)(2,1)S(1)} %fusion.12), channel_id=1, source_target_pairs={{0,16},{16,0},{32,48},{48,32},{64,80},{80,64},{96,112},{112,96},{1... | collective-permute-start | bytes 1572872 | tf_op jit(solution)/shard_map/ppermute | solution.py:19
  292.8 1.5 collective-permute-done.8
  294.3 0.2 add_convert_fusion.1
  294.5 1.9 collective-permute-start.9
  296.4 14.2 %collective-permute-done.9 = bf16[512,512]{1,0:T(8,128)(2,1)S(1)} collective-permute-done((bf16[512,512]{1,0:T(8,128)(2,1)S(1)}, bf16[512,512]{1,0:T(8,128)(2,1)S(1)}, u32[]{:S(2)}, u32[]{:S(2)}) %collective-permute-start.9) | collective-permute-done | bytes 524320 | tf_op jit(solution)/shard_map/ppermute | solution.py:25
  310.6 1.0 fusion.43
  (4 shorter events, 0.1 us)
Async XLA Ops:
  6.5 69.3 %all-gather.5.cloned.1.call-start = ((), (), s32[]{:S(2)}) async-start(), calls=%async_computation | async-start | bytes 5242880 | tf_op jit(solution)/shard_map/all_gather | solution.py:56
  7.3 212.2 %all-gather.7.cloned.1.call-start = ((), (), s32[]{:S(2)}) async-start(), calls=%async_computation.1 | async-start | bytes 5242880 | tf_op jit(solution)/shard_map/all_gather | solution.py:71
  7.3 31.2 %collective-permute-start = (bf16[512,512]{1,0:T(8,128)(2,1)}, bf16[512,512]{1,0:T(8,128)(2,1)S(1)}, u32[]{:S(2)}, u32[]{:S(2)}) collective-permute-start(bf16[512,512]{1,0:T(8,128)(2,1)} %bitcast.100), channel_id=1, source_target_pairs={{0,4},{4,8},{8,12},{12,0},{1,5},{5,9},{9,13},{13,1},{2,6},{6,10},{... | collective-permute-start | bytes 1572872 | tf_op jit(solution)/shard_map/ppermute | solution.py:14
  16.9 54.7 %collective-permute-start.1 = (bf16[512,512]{1,0:T(8,128)(2,1)}, bf16[512,512]{1,0:T(8,128)(2,1)S(1)}, u32[]{:S(2)}, u32[]{:S(2)}) collective-permute-start(bf16[512,512]{1,0:T(8,128)(2,1)} %bitcast.101), channel_id=1, source_target_pairs={{0,12},{4,0},{8,4},{12,8},{1,13},{5,1},{9,5},{13,9},{2,14},{6,2},{... | collective-permute-start | bytes 1572872 | tf_op jit(solution)/shard_map/ppermute | solution.py:14
  22.6 57.3 %copy-start.1 = (bf16[1,1,512,512]{3,2,1,0:T(8,128)(2,1)S(1)}, bf16[1,1,512,512]{3,2,1,0:T(8,128)(2,1)}, u32[]{:S(2)}) copy-start(bf16[1,1,512,512]{3,2,1,0:T(8,128)(2,1)} %param.5) | copy-start | bytes 1572868
  38.5 54.7 %collective-permute-start.2 = (bf16[256,512]{1,0:T(8,128)(2,1)S(1)}, bf16[256,512]{1,0:T(8,128)(2,1)S(1)}, u32[]{:S(2)}, u32[]{:S(2)}) collective-permute-start(bf16[256,512]{1,0:T(8,128)(2,1)S(1)} %slice.48), channel_id=1, source_target_pairs={{0,4},{4,8},{8,12},{12,0},{1,5},{5,9},{9,13},{13,1},{2,6},{6,10},{... | collective-permute-start | bytes 786440 | tf_op jit(solution)/shard_map/ppermute | solution.py:14
  71.7 22.4 %collective-permute-start.3 = (bf16[256,512]{1,0:T(8,128)(2,1)S(1)}, bf16[256,512]{1,0:T(8,128)(2,1)S(1)}, u32[]{:S(2)}, u32[]{:S(2)}) collective-permute-start(bf16[256,512]{1,0:T(8,128)(2,1)S(1)} %slice.49), channel_id=1, source_target_pairs={{0,12},{4,0},{8,4},{12,8},{1,13},{5,1},{9,5},{13,9},{2,14},{6,2},{... | collective-permute-start | bytes 786440 | tf_op jit(solution)/shard_map/ppermute | solution.py:14
  75.8 4.0 %copy-start = (bf16[4,1,2,512,512]{4,3,2,1,0:T(8,128)(2,1)S(1)}, bf16[4,1,2,512,512]{4,3,2,1,0:T(8,128)(2,1)}, u32[]{:S(2)}) copy-start(bf16[4,1,2,512,512]{4,3,2,1,0:T(8,128)(2,1)} %all-gather.5.cloned.1.call-done) | copy-start | bytes 12582916
  95.8 106.1 %collective-permute-start.4 = (bf16[2,512,512]{2,1,0:T(8,128)(2,1)}, bf16[2,512,512]{2,1,0:T(8,128)(2,1)S(1)}, u32[]{:S(2)}, u32[]{:S(2)}) collective-permute-start(bf16[2,512,512]{2,1,0:T(8,128)(2,1)} %bitcast.106), channel_id=1, source_target_pairs={{0,4},{4,8},{8,12},{12,0},{1,5},{5,9},{9,13},{13,1},{2,6},{6,10},{... | collective-permute-start | bytes 3145736 | tf_op jit(solution)/shard_map/ppermute | solution.py:14
  136.3 68.7 %collective-permute-start.5 = (bf16[2,512,512]{2,1,0:T(8,128)(2,1)}, bf16[2,512,512]{2,1,0:T(8,128)(2,1)}, u32[]{:S(2)}, u32[]{:S(2)}) collective-permute-start(bf16[2,512,512]{2,1,0:T(8,128)(2,1)} %bitcast.107), channel_id=1, source_target_pairs={{0,12},{4,0},{8,4},{12,8},{1,13},{5,1},{9,5},{13,9},{2,14},{6,2},{... | collective-permute-start | bytes 3145736 | tf_op jit(solution)/shard_map/ppermute | solution.py:14
  201.9 17.5 %copy-start.3 = (bf16[2,512,512]{2,1,0:T(8,128)(2,1)}, bf16[2,512,512]{2,1,0:T(8,128)(2,1)S(1)}, u32[]{:S(2)}) copy-start(bf16[2,512,512]{2,1,0:T(8,128)(2,1)S(1)} %collective-permute-done.4) | copy-start | bytes 3145732
  202.0 30.9 %collective-permute-start.6 = (bf16[2,256,512]{2,1,0:T(8,128)(2,1)S(1)}, bf16[2,256,512]{2,1,0:T(8,128)(2,1)S(1)}, u32[]{:S(2)}, u32[]{:S(2)}) collective-permute-start(bf16[2,256,512]{2,1,0:T(8,128)(2,1)S(1)} %slice.50), channel_id=1, source_target_pairs={{0,4},{4,8},{8,12},{12,0},{1,5},{5,9},{9,13},{13,1},{2,6},{6,10},{... | collective-permute-start | bytes 1572872 | tf_op jit(solution)/shard_map/ppermute | solution.py:14
  206.1 26.7 %collective-permute-start.7 = (bf16[2,256,512]{2,1,0:T(8,128)(2,1)S(1)}, bf16[2,256,512]{2,1,0:T(8,128)(2,1)}, u32[]{:S(2)}, u32[]{:S(2)}) collective-permute-start(bf16[2,256,512]{2,1,0:T(8,128)(2,1)S(1)} %slice.51), channel_id=1, source_target_pairs={{0,12},{4,0},{8,4},{12,8},{1,13},{5,1},{9,5},{13,9},{2,14},{6,2},{... | collective-permute-start | bytes 1572872 | tf_op jit(solution)/shard_map/ppermute | solution.py:14
  219.5 13.4 %copy-start.5 = (bf16[8,512,512]{2,1,0:T(8,128)(2,1)S(1)}, bf16[8,512,512]{2,1,0:T(8,128)(2,1)}, u32[]{:S(2)}) copy-start(bf16[8,512,512]{2,1,0:T(8,128)(2,1)} %all-gather.7.cloned.1.call-done) | copy-start | bytes 12582916
  221.9 12.7 %copy-start.2 = (f32[1,1,512,512]{3,2,1,0:T(8,128)S(1)}, f32[1,1,512,512]{3,2,1,0:T(8,128)}, u32[]{:S(2)}) copy-start(f32[1,1,512,512]{3,2,1,0:T(8,128)} %param.8) | copy-start | bytes 3145732
  221.9 12.7 %copy-start.4 = (bf16[2,512,512]{2,1,0:T(8,128)(2,1)S(1)}, bf16[2,512,512]{2,1,0:T(8,128)(2,1)}, u32[]{:S(2)}) copy-start(bf16[2,512,512]{2,1,0:T(8,128)(2,1)} %copy-done.3) | copy-start | bytes 3145732
  280.4 13.9 %collective-permute-start.8 = (bf16[512,512]{1,0:T(8,128)(2,1)S(1)}, bf16[512,512]{1,0:T(8,128)(2,1)S(1)}, u32[]{:S(2)}, u32[]{:S(2)}) collective-permute-start(bf16[512,512]{1,0:T(8,128)(2,1)S(1)} %fusion.12), channel_id=1, source_target_pairs={{0,16},{16,0},{32,48},{48,32},{64,80},{80,64},{96,112},{112,96},{1... | collective-permute-start | bytes 1572872 | tf_op jit(solution)/shard_map/ppermute | solution.py:19
  294.5 16.1 %collective-permute-start.9 = (bf16[512,512]{1,0:T(8,128)(2,1)S(1)}, bf16[512,512]{1,0:T(8,128)(2,1)S(1)}, u32[]{:S(2)}, u32[]{:S(2)}) collective-permute-start(bf16[512,512]{1,0:T(8,128)(2,1)S(1)} %add_convert_fusion.1), channel_id=1, source_target_pairs={{0,496},{16,32},{32,16},{48,64},{64,48},{80,96},{96,80},{112,128},... | collective-permute-start | bytes 1572872 | tf_op jit(solution)/shard_map/ppermute | solution.py:25
Sparse Core Ops, SparseCore 0:
  9.4 60.9 all-gather.4
  96.0 123.4 all-gather.6

commit v2 on v1

v2 whole, which is shorter than its diff:
```python
import jax
import jax.numpy as jnp
from jax import lax
from jax.sharding import Mesh
from jax.sharding import PartitionSpec as P


BLOCK = ("block_0", "block_1")
AXES = ("chain", "block_0", "block_1")
SIDE = 4


def permute(value, target):
    chain = lax.axis_size("chain")
    pairs = []
    for seg in range(chain):
        for row in range(SIDE):
            for col in range(SIDE):
                to = target(seg, row, col)
                if to is not None:
                    to_row, to_col = to
                    source = (seg * SIDE + row) * SIDE + col
                    pairs.append((source, (seg * SIDE + to_row) * SIDE + to_col))
    return lax.ppermute(value, AXES, pairs)


def is_active(seg, row):
    return row // 2 == seg % 2


def to_active(seg, row, col):
    return None if is_active(seg, row) else (row ^ 3, col)


def to_home(seg, row, col):
    return (row ^ 3, col) if is_active(seg, row) else None


def to_other(seg, row, col):
    return (row ^ 1, col) if is_active(seg, row) else None


def along_row(value):
    pieces = [value]
    for distance in (1, 2, 3):

        def target(seg, row, col, distance=distance):
            return (row, col ^ distance) if is_active(seg, row) else None

        pieces.append(permute(value, target))
    return jnp.stack(pieces)


def even_partner(value):
    pairs = [(source, source ^ 1) for source in range(lax.axis_size("chain"))]
    return lax.ppermute(value, "chain", pairs)


def odd_partner(value):
    count = lax.axis_size("chain")
    pairs = [(source, (source + (1 if source % 2 else -1)) % count) for source in range(count)]
    return lax.ppermute(value, "chain", pairs)


def after(value, *others):
    return lax.optimization_barrier((value, *others))[0]


def mix_weighted(first_tile, second_tile, first_weight, second_weight):
    return (
        first_weight * first_tile.astype(jnp.float32)
        + second_weight * second_tile.astype(jnp.float32)
    ).astype(jnp.bfloat16)


def one_window(state, left_env, right_env, precond, ranks):
    segment = lax.axis_index("chain")
    row = lax.axis_index("block_0")
    col = lax.axis_index("block_1")
    active = row // 2 == segment % 2
    state_tile = state[0, 0]
    left_tiles = left_env[0, 0]
    right_tiles = right_env[0, 0]
    scaling = precond[0, 0]
    width = state_tile.shape[0]
    half = width // 2
    order_full = SIDE * width

    state_far = permute(state_tile, to_active)
    left_far = permute(left_tiles, to_active)
    state_rows = [
        state_tile,
        permute(state_tile, to_other),
        permute(state_far, to_other),
        state_far,
    ]
    right_other = permute(right_tiles, to_other)
    right_parts = [right_tiles[..., :half], right_tiles[..., half:]]
    right_parts[0] = after(right_parts[0], left_far)
    right_far_0 = permute(right_parts[0], to_active)
    right_parts[1] = after(right_parts[1], right_far_0)
    right_far_1 = permute(right_parts[1], to_active)
    right_cross_0 = permute(right_far_0, to_other)
    right_cross_1 = permute(right_far_1, to_other)
    right_rows = (
        (right_tiles[..., :half], right_other[..., :half], right_cross_0, right_far_0),
        (right_tiles[..., half:], right_other[..., half:], right_cross_1, right_far_1),
    )

    place = col ^ row

    def block_of(stacked, j):
        return lax.dynamic_index_in_dim(stacked, place ^ j, 0, keepdims=False)

    def turn(left_stack):
        total = None
        for j in (0, 1, 3, 2):
            term = jnp.einsum(
                "kij,jl->kil",
                block_of(left_stack, j),
                state_rows[j],
                preferred_element_type=jnp.float32,
            )
            total = term if total is None else total + term
        return total.astype(jnp.bfloat16)

    def apply_right(turned_stack, rows):
        total = None
        for j in (0, 1, 3, 2):
            term = jnp.einsum(
                "kij,kjl->il",
                block_of(turned_stack, j),
                rows[j],
                preferred_element_type=jnp.float32,
            )
            total = term if total is None else total + term
        return total

    turned_own = along_row(turn(along_row(left_tiles)))
    turned_far = along_row(turn(along_row(left_far)))
    home_parts = []
    own_parts = []
    for part in (0, 1):
        far_image = apply_right(turned_far, right_rows[part]).astype(jnp.bfloat16)
        home_parts.append(permute(far_image, to_home))
        own_parts.append(apply_right(turned_own, right_rows[part]))
    image = jnp.where(
        active,
        jnp.concatenate(own_parts, axis=1),
        jnp.concatenate(home_parts, axis=1).astype(jnp.float32),
    )

    state_f = state_tile.astype(jnp.float32)
    row_index = row * width + jnp.arange(width, dtype=jnp.int32)
    col_index = col * width + jnp.arange(width, dtype=jnp.int32)
    rank_limit = ranks[0]
    keep_mask = ((row_index[:, None] < rank_limit) & (col_index[None, :] < rank_limit)).astype(
        jnp.float32
    )
    total_count = float(order_full * order_full)
    weighted = keep_mask * scaling
    state_sq = state_f * state_f
    cross_term = state_f * image
    terms = (
        state_sq,
        cross_term,
        keep_mask * state_sq,
        weighted * state_sq,
        weighted * scaling * state_sq,
        weighted * cross_term,
        weighted * scaling * cross_term,
        weighted * scaling * image * image,
    )
    moments = jnp.stack([jnp.sum(term, axis=0) for term in terms])
    for axis in BLOCK:
        moments = lax.psum(moments, axis)
    moments = jnp.sum(moments, axis=1)
    norm_state, intersection, plain_sq, first_sq, second_sq, first_cross, second_cross, image_sq = (
        moments[index] for index in range(8)
    )
    energy = intersection / norm_state
    corrected = keep_mask * (state_f - (image - energy * state_f) * scaling)
    square_sum = (
        plain_sq
        + 2.0 * energy * first_sq
        + energy * energy * second_sq
        - 2.0 * first_cross
        - 2.0 * energy * second_cross
        + image_sq
    )
    bond = (corrected / jnp.sqrt(square_sum / total_count + 1e-06)).astype(jnp.bfloat16)
    own_pair = mix_weighted(bond, even_partner(bond), 0.75, 0.25)
    result = mix_weighted(own_pair, odd_partner(own_pair), 0.5, 0.5)
    return result[None, None]


def solution(mesh):
    split = Mesh(mesh.devices.reshape(mesh.shape["chain"], SIDE, SIDE), AXES)
    placed = (
        P("chain", BLOCK, None, None),
        P("chain", BLOCK, None, None, None),
        P("chain", BLOCK, None, None, None),
        P("chain", BLOCK, None, None),
        P("chain"),
    )
    return jax.shard_map(
        one_window,
        mesh=split,
        in_specs=placed,
        out_specs=P("chain", BLOCK, None, None),
        check_vma=False,
    )
```

time: 319 us -> 336 us (1.053)
  the two profiles are of different devices: /device:TPU:1 before, /device:TPU:2 now
where the time goes in v2:
time: 336 us; the launch traced here: 335 us
  starting transfers between devices  151 us (45%)
  waiting for transfers between devices  112 us (33%)
  blocking collectives  42.8 us (13%)
  matrix products  13.2 us (4%)
  other arithmetic  7.35 us (2%)
  between operations  6.31 us (2%)
    ppermute x23, starting transfers between devices, permute(): return lax.ppermute(value, AXES, pairs)  121 us
    ppermute x23, waiting for transfers between devices, permute(): return lax.ppermute(value, AXES, pairs)  98.9 us
    psum x2, blocking collectives, one_window(): moments = lax.psum(moments, axis)  42.8 us
    ppermute x1, starting transfers between devices, odd_partner(): return lax.ppermute(value, 'chain', pairs)  25 us
    ppermute x1, waiting for transfers between devices, odd_partner(): return lax.ppermute(value, 'chain', pairs)  11.9 us
    dot_general x16, matrix products, apply_right(): jnp.einsum('kij,kjl->il', block_of(turned_stack, j), rows[j], preferred_e...  7.54 us
  transfers between devices with their start and end apart: 25, of which 10 were waited for; matrix products, arithmetic and copies ran while one was open for 6% of the time, Pallas kernels for 0%

profile of v2, /device:TPU:2, one launch (start us, length us, event | category | flops | bytes accessed | tf_op | source)
XLA Modules:
  0.0 334.9 jit_solution(9164254454218323507)
XLA Ops:
  0.0 3.5 %collective-permute-start.2 = (bf16[2,512,512]{2,1,0:T(8,128)(2,1)}, bf16[2,512,512]{2,1,0:T(8,128)(2,1)}, u32[]{:S(2)}, u32[]{:S(2)}) collective-permute-start(bf16[2,512,512]{2,1,0:T(8,128)(2,1)} %bitcast.220), channel_id=1, source_target_pairs={{0,3},{1,2},{2,1},{3,0},{4,7},{5,6},{6,5},{7,4},{24,27},{25,26},{2... | collective-permute-start | bytes 3145736 | tf_op jit(solution)/shard_map/ppermute | solution.py:24
  3.5 8.4 %collective-permute-start.1 = (bf16[2,512,512]{2,1,0:T(8,128)(2,1)}, bf16[2,512,512]{2,1,0:T(8,128)(2,1)}, u32[]{:S(2)}, u32[]{:S(2)}) collective-permute-start(bf16[2,512,512]{2,1,0:T(8,128)(2,1)} %bitcast.221), channel_id=1, source_target_pairs={{0,2},{1,3},{2,0},{3,1},{4,6},{5,7},{6,4},{7,5},{24,26},{25,27},{2... | collective-permute-start | bytes 3145736 | tf_op jit(solution)/shard_map/ppermute | solution.py:24
  11.9 1.9 collective-permute-start
  13.8 1.3 collective-permute-start.10
  15.1 1.3 collective-permute-start.4
  17.1 1.5 copy.23
  18.8 21.8 %collective-permute-done.4 = bf16[512,512]{1,0:T(8,128)(2,1)S(1)} collective-permute-done((bf16[512,512]{1,0:T(8,128)(2,1)}, bf16[512,512]{1,0:T(8,128)(2,1)S(1)}, u32[]{:S(2)}, u32[]{:S(2)}) %collective-permute-start.4) | collective-permute-done | bytes 524320 | tf_op jit(solution)/shard_map/ppermute | solution.py:24
  40.5 55.7 %collective-permute-start.3 = (bf16[512,512]{1,0:T(8,128)(2,1)S(1)}, bf16[512,512]{1,0:T(8,128)(2,1)S(1)}, u32[]{:S(2)}, u32[]{:S(2)}) collective-permute-start(bf16[512,512]{1,0:T(8,128)(2,1)S(1)} %bitcast.217), channel_id=1, source_target_pairs={{0,4},{1,5},{2,6},{3,7},{4,0},{5,1},{6,2},{7,3},{24,28},{25,29},{2... | collective-permute-start | bytes 1572872 | tf_op jit(solution)/shard_map/ppermute | solution.py:24
  96.3 1.9 collective-permute-start.5
  98.2 2.1 pad_maximum_fusion
  100.4 3.4 %collective-permute-start.17 = (bf16[2,512,512]{2,1,0:T(8,128)(2,1)}, bf16[2,512,512]{2,1,0:T(8,128)(2,1)S(1)}, u32[]{:S(2)}, u32[]{:S(2)}) collective-permute-start(bf16[2,512,512]{2,1,0:T(8,128)(2,1)} %collective-permute-done.10), channel_id=1, source_target_pairs={{0,3},{1,2},{2,1},{3,0},{4,7},{5,6},{6,5},{7,4},{24,27},{25,26},{2... | collective-permute-start | bytes 3145736 | tf_op jit(solution)/shard_map/ppermute | solution.py:24
  103.8 3.0 collective-permute-start.16
  106.8 3.4 %collective-permute-start.15 = (bf16[2,512,512]{2,1,0:T(8,128)(2,1)}, bf16[2,512,512]{2,1,0:T(8,128)(2,1)S(1)}, u32[]{:S(2)}, u32[]{:S(2)}) collective-permute-start(bf16[2,512,512]{2,1,0:T(8,128)(2,1)} %collective-permute-done.10), channel_id=1, source_target_pairs={{0,1},{1,0},{2,3},{3,2},{4,5},{5,4},{6,7},{7,6},{24,25},{25,24},{2... | collective-permute-start | bytes 3145736 | tf_op jit(solution)/shard_map/ppermute | solution.py:24
  110.2 0.7 fusion.57
  110.9 0.7 fusion.53
  111.6 21.5 %collective-permute-done.3 = bf16[512,512]{1,0:T(8,128)(2,1)S(1)} collective-permute-done((bf16[512,512]{1,0:T(8,128)(2,1)S(1)}, bf16[512,512]{1,0:T(8,128)(2,1)S(1)}, u32[]{:S(2)}, u32[]{:S(2)}) %collective-permute-start.3) | collective-permute-done | bytes 524320 | tf_op jit(solution)/shard_map/ppermute | solution.py:24
  133.1 1.3 collective-permute-start.11
  134.4 0.7 fusion.55
  135.1 17.7 %collective-permute-done.5 = bf16[512,512]{1,0:T(8,128)(2,1)S(1)} collective-permute-done((bf16[512,512]{1,0:T(8,128)(2,1)S(1)}, bf16[512,512]{1,0:T(8,128)(2,1)S(1)}, u32[]{:S(2)}, u32[]{:S(2)}) %collective-permute-start.5) | collective-permute-done | bytes 524320 | tf_op jit(solution)/shard_map/ppermute | solution.py:24
  152.8 1.9 collective-permute-start.9
  154.7 0.7 add_convert_fusion.1
  155.4 11.9 %collective-permute-done.11 = bf16[2,512,256]{1,2,0:T(8,128)(2,1)S(1)} collective-permute-done((bf16[2,512,256]{1,2,0:T(8,128)(2,1)S(1)}, bf16[2,512,256]{1,2,0:T(8,128)(2,1)S(1)}, u32[]{:S(2)}, u32[]{:S(2)}) %collective-permute-start.11) | collective-permute-done | bytes 524320 | tf_op jit(solution)/shard_map/ppermute | solution.py:24
  167.4 3.4 %collective-permute-start.8 = (bf16[2,512,512]{2,1,0:T(8,128)(2,1)S(1)}, bf16[2,512,512]{2,1,0:T(8,128)(2,1)S(1)}, u32[]{:S(2)}, u32[]{:S(2)}) collective-permute-start(bf16[2,512,512]{2,1,0:T(8,128)(2,1)S(1)} %add_convert_fusion.1), channel_id=1, source_target_pairs={{0,3},{1,2},{2,1},{3,0},{4,7},{5,6},{6,5},{7,4},{24,27},{25,26},{2... | collective-permute-start | bytes 3145736 | tf_op jit(solution)/shard_map/ppermute | solution.py:24
  170.8 3.0 collective-permute-start.7
  173.8 3.4 %collective-permute-start.6 = (bf16[2,512,512]{2,1,0:T(8,128)(2,1)S(1)}, bf16[2,512,512]{2,1,0:T(8,128)(2,1)S(1)}, u32[]{:S(2)}, u32[]{:S(2)}) collective-permute-start(bf16[2,512,512]{2,1,0:T(8,128)(2,1)S(1)} %add_convert_fusion.1), channel_id=1, source_target_pairs={{0,1},{1,0},{2,3},{3,2},{4,5},{5,4},{6,7},{7,6},{24,25},{25,24},{2... | collective-permute-start | bytes 3145736 | tf_op jit(solution)/shard_map/ppermute | solution.py:24
  177.2 1.3 collective-permute-start.13
  178.5 1.6 pad_maximum_fusion.2
  180.1 0.7 fusion.42
  180.8 0.7 fusion.38
  181.5 0.7 fusion.40
  182.2 0.7 add_convert_fusion
  183.0 12.3 %collective-permute-done.8 = bf16[2,512,512]{2,1,0:T(8,128)(2,1)S(1)} collective-permute-done((bf16[2,512,512]{2,1,0:T(8,128)(2,1)S(1)}, bf16[2,512,512]{2,1,0:T(8,128)(2,1)S(1)}, u32[]{:S(2)}, u32[]{:S(2)}) %collective-permute-start.8) | collective-permute-done | bytes 1048608 | tf_op jit(solution)/shard_map/ppermute | solution.py:24
  195.3 1.9 collective-permute-start.12
  197.2 3.4 %collective-permute-start.20 = (bf16[2,512,512]{2,1,0:T(8,128)(2,1)S(1)}, bf16[2,512,512]{2,1,0:T(8,128)(2,1)S(1)}, u32[]{:S(2)}, u32[]{:S(2)}) collective-permute-start(bf16[2,512,512]{2,1,0:T(8,128)(2,1)S(1)} %add_convert_fusion), channel_id=1, source_target_pairs={{0,3},{1,2},{2,1},{3,0},{4,7},{5,6},{6,5},{7,4},{24,27},{25,26},{2... | collective-permute-start | bytes 3145736 | tf_op jit(solution)/shard_map/ppermute | solution.py:24
  200.6 4.2 %collective-permute-start.19 = (bf16[2,512,512]{2,1,0:T(8,128)(2,1)S(1)}, bf16[2,512,512]{2,1,0:T(8,128)(2,1)S(1)}, u32[]{:S(2)}, u32[]{:S(2)}) collective-permute-start(bf16[2,512,512]{2,1,0:T(8,128)(2,1)S(1)} %add_convert_fusion), channel_id=1, source_target_pairs={{0,2},{1,3},{2,0},{3,1},{4,6},{5,7},{6,4},{7,5},{24,26},{25,27},{2... | collective-permute-start | bytes 3145736 | tf_op jit(solution)/shard_map/ppermute | solution.py:24
  204.9 0.6 pad_maximum_fusion.1
  205.5 2.6 collective-permute-start.18
  208.6 7.8 %collective-permute-start.14 = (bf16[2,512,256]{1,2,0:T(8,128)(2,1)S(1)}, bf16[2,512,256]{1,2,0:T(8,128)(2,1)S(1)}, u32[]{:S(2)}, u32[]{:S(2)}) collective-permute-start(bf16[2,512,256]{1,2,0:T(8,128)(2,1)S(1)} %collective-permute-done.13), channel_id=1, source_target_pairs={{0,4},{1,5},{2,6},{3,7},{4,0},{5,1},{6,2},{7,3},{24,28},{25,29},{2... | collective-permute-start | bytes 1572872 | tf_op jit(solution)/shard_map/ppermute | solution.py:24
  216.9 0.5 convolution_bitcast_fusion.13
  217.4 0.5 convolution_bitcast_fusion.14
  217.8 0.5 fusion.7
  218.8 0.5 fusion.10
  219.3 5.8 %collective-permute-done.20 = bf16[2,512,512]{2,1,0:T(8,128)(2,1)S(1)} collective-permute-done((bf16[2,512,512]{2,1,0:T(8,128)(2,1)S(1)}, bf16[2,512,512]{2,1,0:T(8,128)(2,1)S(1)}, u32[]{:S(2)}, u32[]{:S(2)}) %collective-permute-start.20) | collective-permute-done | bytes 1048608 | tf_op jit(solution)/shard_map/ppermute | solution.py:24
  225.1 4.5 %collective-permute-done.18 = bf16[2,512,512]{2,1,0:T(8,128)(2,1)S(1)} collective-permute-done((bf16[2,512,512]{2,1,0:T(8,128)(2,1)S(1)}, bf16[2,512,512]{2,1,0:T(8,128)(2,1)S(1)}, u32[]{:S(2)}, u32[]{:S(2)}) %collective-permute-start.18) | collective-permute-done | bytes 1048608 | tf_op jit(solution)/shard_map/ppermute | solution.py:24
  229.6 0.5 pad_maximum_fusion.3
  230.1 0.5 convolution_bitcast_fusion.1
  230.6 0.5 convolution_bitcast_fusion.2
  231.1 0.5 fusion.16
  232.1 1.5 collective-permute-start.22
  234.0 0.5 convolution_bitcast_fusion.6
  234.5 0.5 fusion.13
  235.0 0.5 fusion.19
  235.5 1.3 collective-permute-start.21
  236.8 0.5 fusion.11
  237.3 3.4 %collective-permute-done.21 = bf16[512,256]{1,0:T(8,128)(2,1)S(1)} collective-permute-done((bf16[512,256]{1,0:T(8,128)(2,1)S(1)}, bf16[512,256]{1,0:T(8,128)(2,1)S(1)}, u32[]{:S(2)}, u32[]{:S(2)}) %collective-permute-start.21) | collective-permute-done | bytes 262176 | tf_op jit(solution)/shard_map/ppermute | solution.py:24
  240.7 0.9 multiply_reduce_fusion
  241.6 28.3 %psum.14 = f32[8,512]{1,0:T(8,128)S(1)} all-reduce(f32[8,512]{1,0:T(8,128)S(1)} %stack.111), channel_id=1, replica_groups=mesh['chain'=32,'block_0'=4,'block_1'=4] {'block_0'}, use_global_device_ids=true, to_apply=%region_8.9 | all-reduce | flops 4096 | bytes 32768 | tf_op jit(solution)/shard_map/psum | solution.py:176
  269.9 14.5 %psum.15 = f32[8,512]{1,0:T(8,128)S(1)} all-reduce(f32[8,512]{1,0:T(8,128)S(1)} %psum.14), channel_id=1, replica_groups=mesh['chain'=32,'block_0'=4,'block_1'=4] {'block_1'}, use_global_device_ids=true, to_apply=%region_9.10 | all-reduce | flops 4096 | bytes 32768 | tf_op jit(solution)/shard_map/psum | solution.py:176
  284.5 0.7 fusion.126
  290.6 4.7 %collective-permute-start.23 = (bf16[512,512]{1,0:T(8,128)(2,1)S(1)}, bf16[512,512]{1,0:T(8,128)(2,1)S(1)}, u32[]{:S(2)}, u32[]{:S(2)}) collective-permute-start(bf16[512,512]{1,0:T(8,128)(2,1)S(1)} %fusion.23), channel_id=1, source_target_pairs={{0,16},{16,0},{32,48},{48,32},{64,80},{80,64},{96,112},{112,96},{1... | collective-permute-start | bytes 1572872 | tf_op jit(solution)/shard_map/ppermute | solution.py:56
  295.3 1.5 collective-permute-done.23
  297.0 25.0 %collective-permute-start.24 = (bf16[512,512]{1,0:T(8,128)(2,1)S(1)}, bf16[512,512]{1,0:T(8,128)(2,1)S(1)}, u32[]{:S(2)}, u32[]{:S(2)}) collective-permute-start(bf16[512,512]{1,0:T(8,128)(2,1)S(1)} %add_convert_fusion.2), channel_id=1, source_target_pairs={{0,496},{16,32},{32,16},{48,64},{64,48},{80,96},{96,80},{112,128},... | collective-permute-start | bytes 1572872 | tf_op jit(solution)/shard_map/ppermute | solution.py:62
  322.0 11.9 %collective-permute-done.24 = bf16[512,512]{1,0:T(8,128)(2,1)S(1)} collective-permute-done((bf16[512,512]{1,0:T(8,128)(2,1)S(1)}, bf16[512,512]{1,0:T(8,128)(2,1)S(1)}, u32[]{:S(2)}, u32[]{:S(2)}) %collective-permute-start.24) | collective-permute-done | bytes 524320 | tf_op jit(solution)/shard_map/ppermute | solution.py:62
  333.9 1.0 fusion.83
  (32 shorter events, 3.2 us)
Async XLA Ops:
  0.0 98.2 %copy-start.2 = (bf16[1,1,2,512,512]{4,3,2,1,0:T(8,128)(2,1)S(1)}, bf16[1,1,2,512,512]{4,3,2,1,0:T(8,128)(2,1)}, u32[]{:S(2)}) copy-start(bf16[1,1,2,512,512]{4,3,2,1,0:T(8,128)(2,1)} %param.6) | copy-start | bytes 3145732
  0.0 40.5 %copy-start = (bf16[1,1,512,512]{3,2,1,0:T(8,128)(2,1)S(1)}, bf16[1,1,512,512]{3,2,1,0:T(8,128)(2,1)}, u32[]{:S(2)}) copy-start(bf16[1,1,512,512]{3,2,1,0:T(8,128)(2,1)} %param.5) | copy-start | bytes 1572868
  0.0 96.3 %collective-permute-start.2 = (bf16[2,512,512]{2,1,0:T(8,128)(2,1)}, bf16[2,512,512]{2,1,0:T(8,128)(2,1)}, u32[]{:S(2)}, u32[]{:S(2)}) collective-permute-start(bf16[2,512,512]{2,1,0:T(8,128)(2,1)} %bitcast.220), channel_id=1, source_target_pairs={{0,3},{1,2},{2,1},{3,0},{4,7},{5,6},{6,5},{7,4},{24,27},{25,26},{2... | collective-permute-start | bytes 3145736 | tf_op jit(solution)/shard_map/ppermute | solution.py:24
  3.5 94.7 %collective-permute-start.1 = (bf16[2,512,512]{2,1,0:T(8,128)(2,1)}, bf16[2,512,512]{2,1,0:T(8,128)(2,1)}, u32[]{:S(2)}, u32[]{:S(2)}) collective-permute-start(bf16[2,512,512]{2,1,0:T(8,128)(2,1)} %bitcast.221), channel_id=1, source_target_pairs={{0,2},{1,3},{2,0},{3,1},{4,6},{5,7},{6,4},{7,5},{24,26},{25,27},{2... | collective-permute-start | bytes 3145736 | tf_op jit(solution)/shard_map/ppermute | solution.py:24
  11.9 86.3 %collective-permute-start = (bf16[2,512,512]{2,1,0:T(8,128)(2,1)}, bf16[2,512,512]{2,1,0:T(8,128)(2,1)}, u32[]{:S(2)}, u32[]{:S(2)}) collective-permute-start(bf16[2,512,512]{2,1,0:T(8,128)(2,1)} %bitcast.222), channel_id=1, source_target_pairs={{0,1},{1,0},{2,3},{3,2},{4,5},{5,4},{6,7},{7,6},{24,25},{25,24},{2... | collective-permute-start | bytes 3145736 | tf_op jit(solution)/shard_map/ppermute | solution.py:24
  13.8 86.5 %collective-permute-start.10 = (bf16[2,512,512]{2,1,0:T(8,128)(2,1)}, bf16[2,512,512]{2,1,0:T(8,128)(2,1)}, u32[]{:S(2)}, u32[]{:S(2)}) collective-permute-start(bf16[2,512,512]{2,1,0:T(8,128)(2,1)} %bitcast.223), channel_id=1, source_target_pairs={{8,4},{9,5},{10,6},{11,7},{12,0},{13,1},{14,2},{15,3},{16,28},{17,... | collective-permute-start | bytes 3145736 | tf_op jit(solution)/shard_map/ppermute | solution.py:24
  15.1 25.4 %collective-permute-start.4 = (bf16[512,512]{1,0:T(8,128)(2,1)}, bf16[512,512]{1,0:T(8,128)(2,1)S(1)}, u32[]{:S(2)}, u32[]{:S(2)}) collective-permute-start(bf16[512,512]{1,0:T(8,128)(2,1)} %bitcast.216), channel_id=1, source_target_pairs={{8,4},{9,5},{10,6},{11,7},{12,0},{13,1},{14,2},{15,3},{16,28},{17,... | collective-permute-start | bytes 1572872 | tf_op jit(solution)/shard_map/ppermute | solution.py:24
  40.5 92.6 %collective-permute-start.3 = (bf16[512,512]{1,0:T(8,128)(2,1)S(1)}, bf16[512,512]{1,0:T(8,128)(2,1)S(1)}, u32[]{:S(2)}, u32[]{:S(2)}) collective-permute-start(bf16[512,512]{1,0:T(8,128)(2,1)S(1)} %bitcast.217), channel_id=1, source_target_pairs={{0,4},{1,5},{2,6},{3,7},{4,0},{5,1},{6,2},{7,3},{24,28},{25,29},{2... | collective-permute-start | bytes 1572872 | tf_op jit(solution)/shard_map/ppermute | solution.py:24
  96.3 56.5 %collective-permute-start.5 = (bf16[512,512]{1,0:T(8,128)(2,1)S(1)}, bf16[512,512]{1,0:T(8,128)(2,1)S(1)}, u32[]{:S(2)}, u32[]{:S(2)}) collective-permute-start(bf16[512,512]{1,0:T(8,128)(2,1)S(1)} %collective-permute-done.4), channel_id=1, source_target_pairs={{0,4},{1,5},{2,6},{3,7},{4,0},{5,1},{6,2},{7,3},{24,28},{25,29},{2... | collective-permute-start | bytes 1572872 | tf_op jit(solution)/shard_map/ppermute | solution.py:24
  100.4 70.4 %collective-permute-start.17 = (bf16[2,512,512]{2,1,0:T(8,128)(2,1)}, bf16[2,512,512]{2,1,0:T(8,128)(2,1)S(1)}, u32[]{:S(2)}, u32[]{:S(2)}) collective-permute-start(bf16[2,512,512]{2,1,0:T(8,128)(2,1)} %collective-permute-done.10), channel_id=1, source_target_pairs={{0,3},{1,2},{2,1},{3,0},{4,7},{5,6},{6,5},{7,4},{24,27},{25,26},{2... | collective-permute-start | bytes 3145736 | tf_op jit(solution)/shard_map/ppermute | solution.py:24
  103.8 70.0 %collective-permute-start.16 = (bf16[2,512,512]{2,1,0:T(8,128)(2,1)}, bf16[2,512,512]{2,1,0:T(8,128)(2,1)S(1)}, u32[]{:S(2)}, u32[]{:S(2)}) collective-permute-start(bf16[2,512,512]{2,1,0:T(8,128)(2,1)} %collective-permute-done.10), channel_id=1, source_target_pairs={{0,2},{1,3},{2,0},{3,1},{4,6},{5,7},{6,4},{7,5},{24,26},{25,27},{2... | collective-permute-start | bytes 3145736 | tf_op jit(solution)/shard_map/ppermute | solution.py:24
  106.8 70.4 %collective-permute-start.15 = (bf16[2,512,512]{2,1,0:T(8,128)(2,1)}, bf16[2,512,512]{2,1,0:T(8,128)(2,1)S(1)}, u32[]{:S(2)}, u32[]{:S(2)}) collective-permute-start(bf16[2,512,512]{2,1,0:T(8,128)(2,1)} %collective-permute-done.10), channel_id=1, source_target_pairs={{0,1},{1,0},{2,3},{3,2},{4,5},{5,4},{6,7},{7,6},{24,25},{25,24},{2... | collective-permute-start | bytes 3145736 | tf_op jit(solution)/shard_map/ppermute | solution.py:24
  133.1 34.2 %collective-permute-start.11 = (bf16[2,512,256]{1,2,0:T(8,128)(2,1)S(1)}, bf16[2,512,256]{1,2,0:T(8,128)(2,1)S(1)}, u32[]{:S(2)}, u32[]{:S(2)}) collective-permute-start(bf16[2,512,256]{1,2,0:T(8,128)(2,1)S(1)} %get-tuple-element.7), channel_id=1, source_target_pairs={{8,4},{9,5},{10,6},{11,7},{12,0},{13,1},{14,2},{15,3},{16,28},{17,... | collective-permute-start | bytes 1572872 | tf_op jit(solution)/shard_map/ppermute | solution.py:24
  152.8 55.8 %collective-permute-start.9 = (bf16[2,512,512]{1,2,0:T(8,128)(2,1)S(1)}, bf16[2,512,512]{1,2,0:T(8,128)(2,1)S(1)}, u32[]{:S(2)}, u32[]{:S(2)}) collective-permute-start(bf16[2,512,512]{1,2,0:T(8,128)(2,1)S(1)} %bitcast.211), channel_id=1, source_target_pairs={{0,4},{1,5},{2,6},{3,7},{4,0},{5,1},{6,2},{7,3},{24,28},{25,29},{2... | collective-permute-start | bytes 3145736 | tf_op jit(solution)/shard_map/ppermute | solution.py:24
  167.4 27.9 %collective-permute-start.8 = (bf16[2,512,512]{2,1,0:T(8,128)(2,1)S(1)}, bf16[2,512,512]{2,1,0:T(8,128)(2,1)S(1)}, u32[]{:S(2)}, u32[]{:S(2)}) collective-permute-start(bf16[2,512,512]{2,1,0:T(8,128)(2,1)S(1)} %add_convert_fusion.1), channel_id=1, source_target_pairs={{0,3},{1,2},{2,1},{3,0},{4,7},{5,6},{6,5},{7,4},{24,27},{25,26},{2... | collective-permute-start | bytes 3145736 | tf_op jit(solution)/shard_map/ppermute | solution.py:24
  170.8 26.4 %collective-permute-start.7 = (bf16[2,512,512]{2,1,0:T(8,128)(2,1)S(1)}, bf16[2,512,512]{2,1,0:T(8,128)(2,1)S(1)}, u32[]{:S(2)}, u32[]{:S(2)}) collective-permute-start(bf16[2,512,512]{2,1,0:T(8,128)(2,1)S(1)} %add_convert_fusion.1), channel_id=1, source_target_pairs={{0,2},{1,3},{2,0},{3,1},{4,6},{5,7},{6,4},{7,5},{24,26},{25,27},{2... | collective-permute-start | bytes 3145736 | tf_op jit(solution)/shard_map/ppermute | solution.py:24
  173.8 26.8 %collective-permute-start.6 = (bf16[2,512,512]{2,1,0:T(8,128)(2,1)S(1)}, bf16[2,512,512]{2,1,0:T(8,128)(2,1)S(1)}, u32[]{:S(2)}, u32[]{:S(2)}) collective-permute-start(bf16[2,512,512]{2,1,0:T(8,128)(2,1)S(1)} %add_convert_fusion.1), channel_id=1, source_target_pairs={{0,1},{1,0},{2,3},{3,2},{4,5},{5,4},{6,7},{7,6},{24,25},{25,24},{2... | collective-permute-start | bytes 3145736 | tf_op jit(solution)/shard_map/ppermute | solution.py:24
  177.2 28.2 %collective-permute-start.13 = (bf16[2,512,256]{1,2,0:T(8,128)(2,1)S(1)}, bf16[2,512,256]{1,2,0:T(8,128)(2,1)S(1)}, u32[]{:S(2)}, u32[]{:S(2)}) collective-permute-start(bf16[2,512,256]{1,2,0:T(8,128)(2,1)S(1)} %get-tuple-element.8), channel_id=1, source_target_pairs={{8,4},{9,5},{10,6},{11,7},{12,0},{13,1},{14,2},{15,3},{16,28},{17,... | collective-permute-start | bytes 1572872 | tf_op jit(solution)/shard_map/ppermute | solution.py:24
  195.3 23.0 %collective-permute-start.12 = (bf16[2,512,256]{1,2,0:T(8,128)(2,1)S(1)}, bf16[2,512,256]{1,2,0:T(8,128)(2,1)S(1)}, u32[]{:S(2)}, u32[]{:S(2)}) collective-permute-start(bf16[2,512,256]{1,2,0:T(8,128)(2,1)S(1)} %collective-permute-done.11), channel_id=1, source_target_pairs={{0,4},{1,5},{2,6},{3,7},{4,0},{5,1},{6,2},{7,3},{24,28},{25,29},{2... | collective-permute-start | bytes 1572872 | tf_op jit(solution)/shard_map/ppermute | solution.py:24
  197.2 27.9 %collective-permute-start.20 = (bf16[2,512,512]{2,1,0:T(8,128)(2,1)S(1)}, bf16[2,512,512]{2,1,0:T(8,128)(2,1)S(1)}, u32[]{:S(2)}, u32[]{:S(2)}) collective-permute-start(bf16[2,512,512]{2,1,0:T(8,128)(2,1)S(1)} %add_convert_fusion), channel_id=1, source_target_pairs={{0,3},{1,2},{2,1},{3,0},{4,7},{5,6},{6,5},{7,4},{24,27},{25,26},{2... | collective-permute-start | bytes 3145736 | tf_op jit(solution)/shard_map/ppermute | solution.py:24
  200.6 24.5 %collective-permute-start.19 = (bf16[2,512,512]{2,1,0:T(8,128)(2,1)S(1)}, bf16[2,512,512]{2,1,0:T(8,128)(2,1)S(1)}, u32[]{:S(2)}, u32[]{:S(2)}) collective-permute-start(bf16[2,512,512]{2,1,0:T(8,128)(2,1)S(1)} %add_convert_fusion), channel_id=1, source_target_pairs={{0,2},{1,3},{2,0},{3,1},{4,6},{5,7},{6,4},{7,5},{24,26},{25,27},{2... | collective-permute-start | bytes 3145736 | tf_op jit(solution)/shard_map/ppermute | solution.py:24
  205.5 24.1 %collective-permute-start.18 = (bf16[2,512,512]{2,1,0:T(8,128)(2,1)S(1)}, bf16[2,512,512]{2,1,0:T(8,128)(2,1)S(1)}, u32[]{:S(2)}, u32[]{:S(2)}) collective-permute-start(bf16[2,512,512]{2,1,0:T(8,128)(2,1)S(1)} %add_convert_fusion), channel_id=1, source_target_pairs={{0,1},{1,0},{2,3},{3,2},{4,5},{5,4},{6,7},{7,6},{24,25},{25,24},{2... | collective-permute-start | bytes 3145736 | tf_op jit(solution)/shard_map/ppermute | solution.py:24
  208.6 23.0 %collective-permute-start.14 = (bf16[2,512,256]{1,2,0:T(8,128)(2,1)S(1)}, bf16[2,512,256]{1,2,0:T(8,128)(2,1)S(1)}, u32[]{:S(2)}, u32[]{:S(2)}) collective-permute-start(bf16[2,512,256]{1,2,0:T(8,128)(2,1)S(1)} %collective-permute-done.13), channel_id=1, source_target_pairs={{0,4},{1,5},{2,6},{3,7},{4,0},{5,1},{6,2},{7,3},{24,28},{25,29},{2... | collective-permute-start | bytes 1572872 | tf_op jit(solution)/shard_map/ppermute | solution.py:24
  232.1 5.2 %collective-permute-start.22 = (bf16[512,256]{1,0:T(8,128)(2,1)S(1)}, bf16[512,256]{1,0:T(8,128)(2,1)S(1)}, u32[]{:S(2)}, u32[]{:S(2)}) collective-permute-start(bf16[512,256]{1,0:T(8,128)(2,1)S(1)} %fusion.18), channel_id=1, source_target_pairs={{0,12},{1,13},{2,14},{3,15},{4,8},{5,9},{6,10},{7,11},{24,20},{25,... | collective-permute-start | bytes 786440 | tf_op jit(solution)/shard_map/ppermute | solution.py:24
  234.5 6.2 %copy-start.1 = (f32[1,1,512,512]{3,2,1,0:T(8,128)S(1)}, f32[1,1,512,512]{3,2,1,0:T(8,128)}, u32[]{:S(2)}) copy-start(f32[1,1,512,512]{3,2,1,0:T(8,128)} %param.8) | copy-start | bytes 3145732
  235.5 5.2 %collective-permute-start.21 = (bf16[512,256]{1,0:T(8,128)(2,1)S(1)}, bf16[512,256]{1,0:T(8,128)(2,1)S(1)}, u32[]{:S(2)}, u32[]{:S(2)}) collective-permute-start(bf16[512,256]{1,0:T(8,128)(2,1)S(1)} %fusion.19), channel_id=1, source_target_pairs={{0,12},{1,13},{2,14},{3,15},{4,8},{5,9},{6,10},{7,11},{24,20},{25,... | collective-permute-start | bytes 786440 | tf_op jit(solution)/shard_map/ppermute | solution.py:24
  290.6 6.2 %collective-permute-start.23 = (bf16[512,512]{1,0:T(8,128)(2,1)S(1)}, bf16[512,512]{1,0:T(8,128)(2,1)S(1)}, u32[]{:S(2)}, u32[]{:S(2)}) collective-permute-start(bf16[512,512]{1,0:T(8,128)(2,1)S(1)} %fusion.23), channel_id=1, source_target_pairs={{0,16},{16,0},{32,48},{48,32},{64,80},{80,64},{96,112},{112,96},{1... | collective-permute-start | bytes 1572872 | tf_op jit(solution)/shard_map/ppermute | solution.py:56
  297.0 36.9 %collective-permute-start.24 = (bf16[512,512]{1,0:T(8,128)(2,1)S(1)}, bf16[512,512]{1,0:T(8,128)(2,1)S(1)}, u32[]{:S(2)}, u32[]{:S(2)}) collective-permute-start(bf16[512,512]{1,0:T(8,128)(2,1)S(1)} %add_convert_fusion.2), channel_id=1, source_target_pairs={{0,496},{16,32},{32,16},{48,64},{64,48},{80,96},{96,80},{112,128},... | collective-permute-start | bytes 1572872 | tf_op jit(solution)/shard_map/ppermute | solution.py:62
